TPU v7x, 512 devices: a whole 4x8x8 slice. The times are simulated.
512 devices in a mesh: prow: 16 (over z_lo, x, core), pcol: 32 (over y, z_hi).
Axes of the slice: x: 4, y: 8, z: 8 (z_hi: 4, z_lo: 2; z = z_hi * 2 + z_lo), core: 2. Of those that a mesh axis runs over, the one named last changes fastest.
Arguments:
- matrix: float32 [6, 16, 128, 3, 32, 128], P(None, 'prow', None, None, 'pcol'), may hold values from -1 to 40, as said below
- row_codes: int32 [6, 16, 128], P(None, 'prow'), may hold values from 1 to 8
- col_codes: int32 [3, 32, 128], P(None, 'pcol'), may hold values from 1 to 8
- fault_tiles: int32 [96, 2], replicated, may hold values from 0 to 95, as said below
- fault_cells: int32 [96, 2], replicated, may hold values from 0 to 127
- fault_bits: int32 [96], replicated, may hold values from 1 to 2
Outputs:
- factored: float32 [6, 16, 128, 3, 32, 128], P(None, 'prow', None, None, 'pcol')
- col_check: float32 [3, 32, 128], P(None, 'pcol')
- row_check: float32 [6, 16, 128], P(None, 'prow')
- col_flags: float32 [3, 32], P(None, 'pcol')
- row_flags: float32 [6, 16], P(None, 'prow')
Inputs may be any that keep to these rules, and one draw needn't show every extreme that they name: `matrix`: symmetric positive definite. `fault_tiles`: each tile row index appears in exactly one fault, and so does each tile column index.
All inputs are finite; a program needn't handle non-finite values.
Results may differ from a plain program's by a relative error of at most 0.0003.
Values sent between devices are 32-bit elements; how exact they have to be, the bound alone decides.
No kernel may reach another device: no remote copies, remote signals or barrier semaphores. Data moves between devices by JAX's collectives and lax.ppermute only.
A program may use at most 64 MiB of HBM per device.

v0:
```python
import jax
import jax.numpy as jnp
from jax import lax
from jax.sharding import PartitionSpec as P

STEPS = 2
precise = lax.Precision.HIGHEST


def broadcast(block, axis, holder):
    block = jnp.where(lax.axis_index(axis) == holder, block, jnp.zeros_like(block))
    return lax.psum(block, axis)


def factor_diagonal(diagonal):
    factor = jnp.linalg.cholesky(diagonal)
    identity = jnp.eye(diagonal.shape[0], dtype=jnp.float32)
    inverse = jax.scipy.linalg.solve_triangular(factor, identity, lower=True)
    return (factor, inverse)


def form_panel(col_blocks, tile_ids, factor, inverse, step_index):
    product = jnp.einsum("iab,cb->iac", col_blocks, inverse, precision=precise)
    chosen = jnp.where((tile_ids == step_index)[:, None, None], factor[None], 0.0)
    return jnp.where((tile_ids > step_index)[:, None, None], product, chosen)


def update_range(blocks, trailing_rows, trailing_cols):
    update = jnp.einsum("iab,jcb->iajc", trailing_rows, trailing_cols, precision=precise)
    return blocks - update


def local(matrix, row_codes, col_codes, fault_tiles, fault_cells, fault_bits):
    grid_rows = lax.axis_size("prow")
    grid_cols = lax.axis_size("pcol")
    grid_row = lax.axis_index("prow")
    grid_col = lax.axis_index("pcol")
    tile_rows, _, tile_size, tile_cols, _, _ = matrix.shape
    blocks = matrix.reshape(tile_rows, tile_size, tile_cols, tile_size)
    row_weights = row_codes.reshape(tile_rows, tile_size).astype(jnp.float32) * 0.25
    col_weights = col_codes.reshape(tile_cols, tile_size).astype(jnp.float32) * 0.25
    tile_row = jnp.arange(tile_rows, dtype=jnp.int32) * grid_rows + grid_row
    tile_col = jnp.arange(tile_cols, dtype=jnp.int32) * grid_cols + grid_col
    col_check = lax.psum(jnp.einsum("ia,iajc->jc", row_weights, blocks, precision=precise), "prow")
    row_check = lax.psum(jnp.einsum("iajc,jc->ia", blocks, col_weights, precision=precise), "pcol")
    magnitude = jnp.exp2(fault_bits.astype(jnp.float32) - 1.0)
    fault_rows = fault_tiles[:, 0] * tile_size + fault_cells[:, 0]
    fault_cols = fault_tiles[:, 1] * tile_size + fault_cells[:, 1]
    offsets = jnp.arange(tile_size, dtype=jnp.int32)
    local_rows = (tile_row[:, None] * tile_size + offsets[None, :]).reshape(-1)
    local_cols = (tile_col[:, None] * tile_size + offsets[None, :]).reshape(-1)
    hit_rows = (fault_rows[:, None] == local_rows[None, :]).astype(jnp.float32) * magnitude[:, None]
    hit_cols = (fault_cols[:, None] == local_cols[None, :]).astype(jnp.float32)
    faults_added = jnp.dot(hit_rows.T, hit_cols, precision=precise)
    blocks = blocks + faults_added.reshape(tile_rows, tile_size, tile_cols, tile_size)
    picked = (
        jnp.arange(tile_cols, dtype=jnp.int32) * (grid_cols // grid_rows) + grid_col // grid_rows
    )
    owner_row = grid_col % grid_rows

    def factor_panel(blocks, row_check, col_check, step_index):
        root_row = step_index % grid_rows
        root_col = step_index % grid_cols
        local_row = step_index // grid_rows
        local_col = step_index // grid_cols
        diagonal = broadcast(blocks[local_row, :, local_col, :], "prow", root_row)
        factor, inverse = factor_diagonal(diagonal)
        own_rows = form_panel(blocks[:, :, local_col, :], tile_row, factor, inverse, step_index)
        own_check = jnp.dot(inverse, col_check[local_col], precision=precise)
        panel_rows, new_check = (
            broadcast(own_rows, "pcol", root_col),
            broadcast(own_check, "pcol", root_col),
        )
        across = broadcast(jnp.take(panel_rows, picked, axis=0), "prow", owner_row)
        owner_col = grid_col == root_col
        shift_term = jnp.einsum("jab,ja->b", across, col_weights, precision=precise)
        shift_term = shift_term - jnp.where(owner_col, col_weights[local_col], 0.0)
        shift_vector = lax.psum(shift_term, "pcol")
        row_check = row_check - jnp.einsum("iab,b->ia", panel_rows, shift_vector, precision=precise)
        col_update = jnp.einsum("jab,b->ja", across, new_check, precision=precise)
        col_check = col_check - jnp.where((tile_col > step_index)[:, None], col_update, 0.0)
        col_check = col_check.at[local_col].set(
            jnp.where(owner_col, new_check, col_check[local_col])
        )
        trailing_rows = jnp.where((tile_row > step_index)[:, None, None], panel_rows, 0.0)
        trailing_cols = jnp.where((tile_col > step_index)[:, None, None], across, 0.0)
        return (panel_rows, trailing_rows, trailing_cols, row_check, col_check)

    current = factor_panel(blocks, row_check, col_check, 0)
    for step_index in range(STEPS):
        panel_rows, trailing_rows, trailing_cols, row_check, col_check = current
        blocks = update_range(blocks, trailing_rows, trailing_cols)
        if step_index + 1 < STEPS:
            current = factor_panel(blocks, row_check, col_check, step_index + 1)
        settle_blocks = blocks
        settle_local_col = step_index // grid_cols
        previous = settle_blocks[:, :, settle_local_col, :]
        settle_blocks = settle_blocks.at[:, :, settle_local_col, :].set(
            jnp.where(grid_col == step_index % grid_cols, panel_rows, previous)
        )
        cleared = (tile_row == step_index)[:, None, None, None] & (tile_col > step_index)[
            None, None, :, None
        ]
        blocks = jnp.where(cleared, 0.0, settle_blocks)
    col_found = lax.psum(jnp.einsum("ia,iajc->jc", row_weights, blocks, precision=precise), "prow")
    row_found = lax.psum(jnp.einsum("iajc,jc->ia", blocks, col_weights, precision=precise), "pcol")
    col_flags = jnp.max(jnp.abs(col_check - col_found), axis=1)
    row_flags = jnp.max(jnp.abs(row_check - row_found), axis=1)
    return (
        blocks.reshape(matrix.shape),
        col_check.reshape(tile_cols, 1, tile_size),
        row_check.reshape(tile_rows, 1, tile_size),
        col_flags.reshape(tile_cols, 1),
        row_flags.reshape(tile_rows, 1),
    )


def solution(mesh):
    return jax.shard_map(
        local,
        mesh=mesh,
        in_specs=(
            P(None, "prow", None, None, "pcol", None),
            P(None, "prow", None),
            P(None, "pcol", None),
            P(),
            P(),
            P(),
        ),
        out_specs=(
            P(None, "prow", None, None, "pcol", None),
            P(None, "pcol", None),
            P(None, "prow", None),
            P(None, "pcol"),
            P(None, "prow"),
        ),
        check_vma=False,
    )
```

profile of v0, /device:TPU:64, one launch (start us, length us, event | category | flops | bytes accessed | tf_op | source)
XLA Modules:
  0.0 1383.4 jit_solution(15013393687045354452)
XLA Ops:
  7.2 0.7 multiply_exponential_fusion
  8.1 0.8 add_bitcast_fusion.2
  8.8 0.7 fusion.15
  9.6 1.3 reshape.353
  10.9 0.3 copy-done.7
  11.2 0.9 copy.30
  12.1 1.7 bitcast_add_fusion
  13.8 0.6 fusion.42
  14.6 0.6 broadcast_compare_fusion.4
  15.2 0.6 broadcast_and_fusion
  15.9 118.3 %all-reduce.9.cloned.1.call-done = f32[128,128]{0,1:T(8,128)} async-done(((f32[128,128]{0,1:T(8,128)}), f32[128,128]{0,1:T(8,128)}) %all-reduce.9.cloned.1.call-update) | async-done | bytes 65552 | tf_op jit(solution)/shard_map/psum | solution.py:12
  134.2 0.9 copy.33
  135.1 0.9 fusion.48
  135.9 11.7 cholesky.44
  147.7 0.6 compare_reduce_fusion.1
  148.3 0.7 select_bitcast_fusion.1
  149.0 9.8 custom-call.6
  158.8 0.3 fusion.37
  159.2 1.2 fusion.1
  160.6 0.7 fusion.2
  161.3 309.4 %all-reduce.11.cloned.1.call-done = f32[6,128,128]{1,2,0:T(8,128)} async-done(((f32[6,128,128]{1,2,0:T(8,128)}), f32[6,128,128]{1,2,0:T(8,128)}) %all-reduce.11.cloned.1.call-update) | async-done | bytes 393232 | tf_op jit(solution)/shard_map/psum | solution.py:12
  470.7 1.6 gather_fusion
  472.2 0.8 select_select_fusion.1
  473.1 0.7 broadcast_and_fusion.1
  473.8 118.5 %all-reduce.13.cloned.1.call-done = f32[3,128,128]{1,2,0:T(8,128)} async-done(((f32[3,128,128]{1,2,0:T(8,128)}), f32[3,128,128]{1,2,0:T(8,128)}) %all-reduce.13.cloned.1.call-update) | async-done | bytes 196624 | tf_op jit(solution)/shard_map/psum | solution.py:12
  592.2 2.3 convolution_subtract_fusion.1
  594.6 0.6 fusion.41
  595.2 0.2 all-reduce.17.cloned.1.call-start
  595.5 1.7 convolution_reduce_fusion.1
  597.2 115.8 %all-reduce.15.cloned.1.call-done = f32[128,128]{0,1:T(8,128)} async-done(((f32[128,128]{0,1:T(8,128)}), f32[128,128]{0,1:T(8,128)}) %all-reduce.15.cloned.1.call-update) | async-done | bytes 65552 | tf_op jit(solution)/shard_map/psum | solution.py:12
  712.9 0.9 copy.42
  713.9 0.9 fusion.45
  714.7 11.7 cholesky.55
  726.5 0.6 compare_reduce_fusion
  727.1 0.7 select_bitcast_fusion
  727.8 9.8 custom-call.7
  737.6 0.3 fusion.35
  738.0 1.2 fusion
  739.4 0.8 fusion.7
  740.2 309.2 %all-reduce.17.cloned.1.call-done = f32[6,128,128]{1,2,0:T(8,128)} async-done(((f32[6,128,128]{1,2,0:T(8,128)}), f32[6,128,128]{1,2,0:T(8,128)}) %all-reduce.17.cloned.1.call-update) | async-done | bytes 393232 | tf_op jit(solution)/shard_map/psum | solution.py:12
  1049.4 1.7 gather_fusion.1
  1051.2 0.8 select_select_fusion
  1052.0 119.1 %all-reduce.19.cloned.1.call-done = f32[3,128,128]{1,2,0:T(8,128)} async-done(((f32[3,128,128]{1,2,0:T(8,128)}), f32[3,128,128]{1,2,0:T(8,128)}) %all-reduce.19.cloned.1.call-update) | async-done | bytes 196624 | tf_op jit(solution)/shard_map/psum | solution.py:12
  1171.1 2.2 convolution_subtract_fusion
  1173.4 0.6 copy-done.15
  1174.1 0.1 fusion.93
  1174.3 0.5 copy-done.14
  1174.8 1.1 convolution_reduce_fusion
  1176.0 30.0 %all-reduce.1 = (f32[3,128]{1,0:T(4,128)S(1)}, f32[3,128]{1,0:T(4,128)S(1)}) all-reduce(f32[3,128]{1,0:T(4,128)S(1)} %bitcast.205, f32[3,128]{1,0:T(4,128)S(1)} %bitcast.206), channel_id=1, replica_groups=mesh['prow'=16,'pcol'=32] {'prow'}, use_global_device_ids=true, to_apply=%region_8.12 | all-reduce | flops 768 | bytes 6144 | tf_op jit(solution)/shard_map/psum | solution.py:44
  1206.0 0.2 fusion.5
  1206.2 83.8 %psum.105 = f32[128]{0:T(128)S(1)} all-reduce(f32[128]{0:T(128)S(1)} %fusion.5), channel_id=1, replica_groups=mesh['prow'=16,'pcol'=32] {'pcol'}, use_global_device_ids=true, to_apply=%region_9.13 | all-reduce | flops 128 | bytes 1024 | tf_op jit(solution)/shard_map/psum | solution.py:12
  1290.0 0.2 fusion.71
  1290.3 0.2 fusion.4
  1290.5 0.8 fusion.56
  1291.3 2.6 copy.50
  1294.0 0.3 fusion.6
  1294.2 78.9 %all-reduce = (f32[128]{0:T(128)S(1)}, f32[6,128]{1,0:T(8,128)S(1)}, f32[128]{0:T(128)S(1)}, f32[128]{0:T(128)S(1)}, f32[6,128]{1,0:T(8,128)S(1)}) all-reduce(f32[128]{0:T(128)S(1)} %fusion.4, f32[6,128]{1,0:T(8,128)S(1)} %bitcast.203, f32[128]{0:T(128)S(1)} %fusion.6, ...), channel_id=1, replica_groups=mesh['prow'=16,'pcol'=32] {'pcol'}, use_global_device_ids=true, to_apply=%region_10.14 | all-reduce | flops 1920 | bytes 15360 | tf_op jit(solution)/shard_map/psum | solution.py:12
  1373.2 0.2 fusion.68
  1373.5 0.6 reshape.358
  1374.1 0.6 abs_reduce_fusion.1
  1374.7 0.3 fusion.66
  1375.0 0.3 fusion.64
  1375.3 0.7 abs_reduce_fusion
  1376.0 0.6 reshape.359
  (95 shorter events, 1.4 us)
Async XLA Ops:
  7.2 127.0 %all-reduce.9.cloned.1.call-start = ((), (), s32[]{:S(2)}) async-start(), calls=%async_computation | async-start | bytes 131072 | tf_op jit(solution)/shard_map/psum | solution.py:12
  9.6 1.7 copy-start.7
  12.1 3.1 copy-start.12
  14.5 456.2 %all-reduce.11.cloned.1.call-start = ((), (), s32[]{:S(2)}) async-start(), calls=%async_computation.1 | async-start | bytes 786432 | tf_op jit(solution)/shard_map/psum | solution.py:12
  14.6 1.3 copy-start.20
  14.6 458.5 %copy-start.18 = (pred[3]{0:T(512)(128)(4,1)}, pred[3]{0:T(512)(128)(4,1)S(1)}, u32[]{:S(2)}) copy-start(pred[3]{0:T(512)(128)(4,1)S(1)} %broadcast_compare_fusion.3) | copy-start | bytes 13
  14.6 146.6 %copy-start.29 = (pred[6]{0:T(512)(128)(4,1)}, pred[6]{0:T(512)(128)(4,1)S(1)}, u32[]{:S(2)}) copy-start(pred[6]{0:T(512)(128)(4,1)S(1)} %get-tuple-element.81) | copy-start | bytes 22
  15.2 457.9 %copy-start.27 = (pred[6]{0:T(512)(128)(4,1)}, pred[6]{0:T(512)(128)(4,1)S(1)}, u32[]{:S(2)}) copy-start(pred[6]{0:T(512)(128)(4,1)S(1)} %get-tuple-element.84) | copy-start | bytes 22
  15.9 456.4 %copy-start.24 = (pred[3]{0:T(512)(128)(4,1)}, pred[3]{0:T(512)(128)(4,1)S(1)}, u32[]{:S(2)}) copy-start(pred[3]{0:T(512)(128)(4,1)S(1)} %compare_and_fusion) | copy-start | bytes 13
  159.1 2.2 copy-start.8
  160.5 431.8 %all-reduce.13.cloned.1.call-start = ((), (), s32[]{:S(2)}) async-start(), calls=%async_computation.2 | async-start | bytes 393216 | tf_op jit(solution)/shard_map/psum | solution.py:12
  160.6 313.2 %copy-start.17 = (s32[1024]{0:T(1024)}, s32[1024]{0:T(1024)S(1)}, u32[]{:S(2)}) copy-start(s32[1024]{0:T(1024)S(1)} %pad_clamp_fusion) | copy-start | bytes 12292
  473.0 239.9 %all-reduce.15.cloned.1.call-start = ((), (), s32[]{:S(2)}) async-start(), calls=%async_computation.3 | async-start | bytes 131072 | tf_op jit(solution)/shard_map/psum | solution.py:12
  473.8 121.7 %copy-start.13 = (s32[6,1,128]{2,1,0:T(1,128)S(1)}, s32[6,1,128]{2,1,0:T(1,128)}, u32[]{:S(2)}) copy-start(s32[6,1,128]{2,1,0:T(1,128)} %param.20) | copy-start | bytes 9220
  594.6 143.4 %copy-start.23 = (pred[6]{0:T(512)(128)(4,1)S(1)}, pred[6]{0:T(512)(128)(4,1)}, u32[]{:S(2)}) copy-start(pred[6]{0:T(512)(128)(4,1)} %get-tuple-element.83) | copy-start | bytes 22
  594.6 143.4 %copy-start.28 = (pred[6]{0:T(512)(128)(4,1)S(1)}, pred[6]{0:T(512)(128)(4,1)}, u32[]{:S(2)}) copy-start(pred[6]{0:T(512)(128)(4,1)} %copy-done.27) | copy-start | bytes 22
  595.2 454.2 %all-reduce.17.cloned.1.call-start = ((), (), s32[]{:S(2)}) async-start(), calls=%async_computation.4 | async-start | bytes 786432 | tf_op jit(solution)/shard_map/psum | solution.py:12
  597.2 142.2 %copy-start.5 = (f32[3,128,128]{1,2,0:T(8,128)S(1)}, f32[3,128,128]{1,2,0:T(8,128)}, u32[]{:S(2)}) copy-start(f32[3,128,128]{1,2,0:T(8,128)} %all-reduce.13.cloned.1.call-done) | copy-start | bytes 589828
  737.9 1.4 copy-start.10
  738.0 313.2 %copy-start.25 = (pred[3]{0:T(512)(128)(4,1)S(1)}, pred[3]{0:T(512)(128)(4,1)}, u32[]{:S(2)}) copy-start(pred[3]{0:T(512)(128)(4,1)} %copy-done.24) | copy-start | bytes 13
  739.3 312.7 %copy-start.2 = (f32[6,128,128]{1,2,0:T(8,128)S(1)}, f32[6,128,128]{1,2,0:T(8,128)}, u32[]{:S(2)}) copy-start(f32[6,128,128]{1,2,0:T(8,128)} %all-reduce.11.cloned.1.call-done) | copy-start | bytes 1179652
  739.3 431.8 %all-reduce.19.cloned.1.call-start = ((), (), s32[]{:S(2)}) async-start(), calls=%async_computation.5 | async-start | bytes 393216 | tf_op jit(solution)/shard_map/psum | solution.py:12
  740.2 430.9 %copy-start.19 = (pred[3]{0:T(512)(128)(4,1)S(1)}, pred[3]{0:T(512)(128)(4,1)}, u32[]{:S(2)}) copy-start(pred[3]{0:T(512)(128)(4,1)} %copy-done.18) | copy-start | bytes 13
  740.2 430.9 %copy-start.22 = (pred[6,3]{1,0:T(8,128)(4,1)S(1)}, pred[6,3]{1,0:T(8,128)(4,1)}, u32[]{:S(2)}) copy-start(pred[6,3]{1,0:T(8,128)(4,1)} %broadcast_and_fusion) | copy-start | bytes 58
  1049.4 121.7 %copy-start = (f32[6,128,128]{1,2,0:T(8,128)S(1)}, f32[6,128,128]{1,2,0:T(8,128)}, u32[]{:S(2)}) copy-start(f32[6,128,128]{1,2,0:T(8,128)} %all-reduce.17.cloned.1.call-done) | copy-start | bytes 1179652
  1173.3 0.7 copy-start.15
  1174.1 0.7 copy-start.14
  1174.3 1.6 copy-start.16
  1174.3 31.7 %copy-start.9 = (f32[128,128]{1,0:T(8,128)S(1)}, f32[128,128]{1,0:T(8,128)}, u32[]{:S(2)}) copy-start(f32[128,128]{1,0:T(8,128)} %copy-done.8) | copy-start | bytes 196612
  1174.3 115.7 %copy-start.6 = (f32[3,128,128]{1,2,0:T(8,128)S(1)}, f32[3,128,128]{1,2,0:T(8,128)}, u32[]{:S(2)}) copy-start(f32[3,128,128]{1,2,0:T(8,128)} %all-reduce.13.cloned.1.call-done) | copy-start | bytes 589828
  1174.3 115.9 %copy-start.21 = (pred[3]{0:T(512)(128)(4,1)S(1)}, pred[3]{0:T(512)(128)(4,1)}, u32[]{:S(2)}) copy-start(pred[3]{0:T(512)(128)(4,1)} %copy-done.20) | copy-start | bytes 13
  1174.3 116.0 %copy-start.11 = (f32[128,128]{1,0:T(8,128)S(1)}, f32[128,128]{1,0:T(8,128)}, u32[]{:S(2)}) copy-start(f32[128,128]{1,0:T(8,128)} %copy-done.10) | copy-start | bytes 196612
  1291.2 2.7 copy-start.4
  1291.2 3.0 copy-start.26
  1291.3 83.5 %copy-start.3 = (f32[6,128,128]{1,2,0:T(8,128)S(1)}, f32[6,128,128]{1,2,0:T(8,128)}, u32[]{:S(2)}) copy-start(f32[6,128,128]{1,2,0:T(8,128)} %all-reduce.11.cloned.1.call-done) | copy-start | bytes 1179652
  1291.3 83.8 %copy-start.1 = (f32[6,128,128]{1,2,0:T(8,128)S(1)}, f32[6,128,128]{1,2,0:T(8,128)}, u32[]{:S(2)}) copy-start(f32[6,128,128]{1,2,0:T(8,128)} %all-reduce.17.cloned.1.call-done) | copy-start | bytes 1179652
Sparse Core Ops, SparseCore 0:
  14.6 119.4 all-reduce.8
  160.6 310.0 all-reduce.10
  474.2 118.0 all-reduce.12
  595.8 117.0 all-reduce.14
  739.4 309.9 all-reduce.16
  1053.0 118.0 all-reduce.18
where the time goes:
time: 1380 us
  waiting for transfers between devices  1090 us (79%)
  blocking collectives  193 us (14%)
  other arithmetic  57.3 us (4%)
  matrix products  15.1 us (1%)
  between operations  14.7 us (1%)
    psum x6, waiting for transfers between devices, broadcast(): return lax.psum(block, axis)  1090 us
    psum x2, blocking collectives, broadcast(): return lax.psum(block, axis)  163 us
    psum x1, blocking collectives, local(): lax.psum(jnp.einsum('ia,iajc->jc', row_weights, blocks, precision=precise...  30 us
  transfers between devices with their start and end apart: 6, of which 6 were waited for; matrix products, arithmetic and copies ran while one was open for 0% of the time, Pallas kernels for 0%

commit v1 on v0

--- a/solution.py
+++ b/solution.py
@@ -9,7 +9,7 @@
 
 def broadcast(block, axis, holder):
     block = jnp.where(lax.axis_index(axis) == holder, block, jnp.zeros_like(block))
-    return lax.psum(block, axis)
+    return jnp.sum(lax.all_gather(block, axis), axis=0)
 
 
 def factor_diagonal(diagonal):

time: 1380 us -> 884 us (0.64)
  waiting for transfers between devices: 1090 us -> 507 us
  blocking collectives: 193 us -> 268 us
  other arithmetic: 57.3 us -> 72.1 us
    psum x6 -> x0, waiting for transfers between devices: 1090 us -> none  [broadcast(): return lax.psum(block, axis)]
    all_gather x0 -> x6, waiting for transfers between devices: none -> 507 us  [broadcast(): return jnp.sum(lax.all_gather(block, axis), axis=0)]
    all_gather x0 -> x2, blocking collectives: none -> 156 us  [broadcast(): return jnp.sum(lax.all_gather(block, axis), axis=0)]
    psum x2 -> x1, blocking collectives: 163 us -> 81.7 us  [local(): lax.psum(jnp.einsum('iajc,jc->ia', blocks, col_weights, precision=precise...]
    reduce_sum x0 -> x8, other arithmetic: none -> 17.3 us  [broadcast(): return jnp.sum(lax.all_gather(block, axis), axis=0)]
  transfers between devices with their start and end apart: 6 -> 6, of which waited for: 6 -> 6; matrix products, arithmetic and copies ran while one was open for 0% -> 1% of each run, Pallas kernels for 0% -> 0%
where the time goes in v1:
time: 884 us
  waiting for transfers between devices  507 us (57%)
  blocking collectives  268 us (30%)
  other arithmetic  72.1 us (8%)
  between operations  14.7 us (2%)
  matrix products  14.6 us (2%)
    all_gather x6, waiting for transfers between devices, broadcast(): return jnp.sum(lax.all_gather(block, axis), axis=0)  507 us
    all_gather x2, blocking collectives, broadcast(): return jnp.sum(lax.all_gather(block, axis), axis=0)  156 us
    psum x1, blocking collectives, local(): lax.psum(jnp.einsum('iajc,jc->ia', blocks, col_weights, precision=precise...  81.7 us
    psum x1, blocking collectives, local(): lax.psum(jnp.einsum('ia,iajc->jc', row_weights, blocks, precision=precise...  29.6 us
    another operation x6, other arithmetic, factor_diagonal(): factor = jnp.linalg.cholesky(diagonal)  24.8 us
    another operation x4, other arithmetic, factor_diagonal(): inverse = jax.scipy.linalg.solve_triangular(factor, identity, lower=True)  20.9 us
  transfers between devices with their start and end apart: 6, of which 6 were waited for; matrix products, arithmetic and copies ran while one was open for 1% of the time, Pallas kernels for 0%

profile of v1, /device:TPU:64, one launch (start us, length us, event | category | flops | bytes accessed | tf_op | source)
XLA Modules:
  0.0 883.7 jit_solution(9732632453904174821)
XLA Ops:
  7.4 0.7 multiply_exponential_fusion
  8.0 0.8 add_bitcast_fusion.2
  8.8 0.7 fusion.30
  9.6 0.2 reshape.373
  9.7 1.4 copy.30
  11.2 1.4 bitcast_add_fusion
  12.6 0.7 fusion.57
  13.5 41.4 %all-gather.17.cloned.1.call-done = f32[16,128,1,128]{3,1,2,0:T(8,128)} async-done(((f32[1,128,1,128]{3,1,2,0:T(8,128)}), f32[16,128,1,128]{3,1,2,0:T(8,128)}) %all-gather.17.cloned.1.call-update) | async-done | bytes 1048592 | tf_op jit(solution)/shard_map/all_gather | solution.py:12
  54.9 1.3 bitcast_reduce_fusion.1
  56.3 11.7 %cholesky.44 = f32[128,128]{1,0:T(8,128)S(1)} custom-call(f32[128,128]{1,0:T(8,128)S(1)} %fusion.63), custom_call_target="Cholesky" | custom-call | tf_op jit(solution)/shard_map/jit(cholesky)/cholesky | solution.py:16
  68.0 0.6 compare_reduce_fusion.1
  68.7 0.7 select_bitcast_fusion.2
  69.3 9.8 %custom-call.6 = f32[1,128,128]{1,2,0:T(8,128)S(1)} custom-call(f32[1,128,128]{2,1,0:T(8,128)S(1)} %get-tuple-element.81), custom_call_target="InvertDiagBlocksLowerTriangular" | custom-call | tf_op jit(solution)/shard_map/jit(_solve_triangular)/triangular_solve | solution.py:18
  79.1 0.3 fusion.52
  79.4 1.3 fusion.1
  80.8 179.4 %all-gather.19.cloned.1.call-done = f32[192,128,128]{2,1,0:T(8,128)} async-done(((f32[6,128,128]{2,1,0:T(8,128)}), f32[192,128,128]{2,1,0:T(8,128)}) %all-gather.19.cloned.1.call-update) | async-done | bytes 12582928 | tf_op jit(solution)/shard_map/all_gather | solution.py:12
  260.3 5.3 reduce_sum.81
  265.5 0.6 gather_fusion
  266.1 0.8 select_select_fusion.1
  267.0 36.6 %all-gather.21.cloned.1.call-done = f32[48,128,128]{2,1,0:T(8,128)} async-done(((f32[3,128,128]{2,1,0:T(8,128)}), f32[48,128,128]{2,1,0:T(8,128)}) %all-gather.21.cloned.1.call-update) | async-done | bytes 3145744 | tf_op jit(solution)/shard_map/all_gather | solution.py:12
  303.6 2.1 reduce_sum.82
  305.6 2.4 convolution_subtract_fusion.1
  308.1 0.6 fusion.56
  308.7 0.2 all-gather.25.cloned.1.call-start
  309.0 37.7 %all-gather.23.cloned.1.call-done = f32[16,128,1,128]{3,1,2,0:T(8,128)} async-done(((f32[1,128,1,128]{3,1,2,0:T(8,128)}), f32[16,128,1,128]{3,1,2,0:T(8,128)}) %all-gather.23.cloned.1.call-update) | async-done | bytes 1048592 | tf_op jit(solution)/shard_map/all_gather | solution.py:12
  346.7 1.3 bitcast_reduce_fusion
  348.1 11.7 %cholesky.55 = f32[128,128]{1,0:T(8,128)S(1)} custom-call(f32[128,128]{1,0:T(8,128)S(1)} %fusion.60), custom_call_target="Cholesky" | custom-call | tf_op jit(solution)/shard_map/jit(cholesky)/cholesky | solution.py:16
  359.9 0.6 compare_reduce_fusion
  360.5 0.7 select_bitcast_fusion.1
  361.2 9.8 %custom-call.7 = f32[1,128,128]{1,2,0:T(8,128)S(1)} custom-call(f32[1,128,128]{2,1,0:T(8,128)S(1)} %get-tuple-element.79), custom_call_target="InvertDiagBlocksLowerTriangular" | custom-call | tf_op jit(solution)/shard_map/jit(_solve_triangular)/triangular_solve | solution.py:18
  371.0 0.3 fusion.50
  371.3 1.2 fusion
  372.6 179.5 %all-gather.25.cloned.1.call-done = f32[192,128,128]{2,1,0:T(8,128)} async-done(((f32[6,128,128]{2,1,0:T(8,128)}), f32[192,128,128]{2,1,0:T(8,128)}) %all-gather.25.cloned.1.call-update) | async-done | bytes 12582928 | tf_op jit(solution)/shard_map/all_gather | solution.py:12
  552.1 5.3 reduce_sum.85
  557.4 0.6 gather_fusion.1
  557.9 0.8 select_select_fusion
  558.8 0.7 fusion.5
  559.4 0.6 copy.82
  560.0 1.0 fusion.2
  561.2 0.6 broadcast_and_fusion
  561.8 0.7 broadcast_and_fusion.1
  562.4 0.8 fusion.13
  563.3 32.1 %all-gather.27.cloned.1.call-done = f32[48,128,128]{2,1,0:T(8,128)} async-done(((f32[3,128,128]{2,1,0:T(8,128)}), f32[48,128,128]{2,1,0:T(8,128)}) %all-gather.27.cloned.1.call-update) | async-done | bytes 3145744 | tf_op jit(solution)/shard_map/all_gather | solution.py:12
  595.4 2.1 reduce_sum.86
  597.4 1.9 convolution_subtract_fusion
  599.5 0.5 copy-done.9
  600.0 0.7 fusion.16
  600.8 29.6 %all-reduce.1 = (f32[3,128]{1,0:T(4,128)S(1)}, f32[3,128]{1,0:T(4,128)}) all-reduce(f32[3,128]{1,0:T(4,128)S(1)} %bitcast.207, f32[3,128]{1,0:T(4,128)S(1)} %bitcast.208), channel_id=1, replica_groups=mesh['prow'=16,'pcol'=32] {'prow'}, use_global_device_ids=true, to_apply=%region_8.12 | all-reduce | flops 768 | bytes 6144 | tf_op jit(solution)/shard_map/psum | solution.py:44
  630.4 0.2 fusion.10
  630.6 81.4 %all-gather.8 = f32[32,1,128]{2,1,0:T(1,128)S(1)} all-gather(f32[1,1,128]{2,1,0:T(1,128)S(1)} %fusion.10), channel_id=8, replica_groups=mesh['prow'=16,'pcol'=32] {'pcol'}, dimensions={0}, use_global_device_ids=true | all-gather | bytes 16896 | tf_op jit(solution)/shard_map/all_gather | solution.py:12
  712.0 0.3 fusion.86
  712.4 0.2 fusion.11
  712.6 1.2 fusion.14
  713.8 0.2 fusion.12
  714.2 74.9 %all-gather.9 = f32[32,1,128]{2,1,0:T(1,128)S(1)} all-gather(f32[1,1,128]{2,1,0:T(1,128)S(1)} %fusion.11), channel_id=9, replica_groups=mesh['prow'=16,'pcol'=32] {'pcol'}, dimensions={0}, use_global_device_ids=true | all-gather | bytes 16896 | tf_op jit(solution)/shard_map/all_gather | solution.py:12
  789.1 0.3 fusion.83
  789.6 81.7 %all-reduce = (f32[6,128]{1,0:T(8,128)S(1)}, f32[128]{0:T(128)S(1)}, f32[128]{0:T(128)S(1)}, f32[6,128]{1,0:T(8,128)S(1)}) all-reduce(f32[6,128]{1,0:T(8,128)S(1)} %bitcast.205, f32[128]{0:T(128)S(1)} %fusion.12, f32[128]{0:T(128)S(1)} %copy-done.12, f32[6,128]{1,0:T(8,128)S(1)} %bitcast.206), channel_id=1, replica_groups=mesh['prow'=16,'pcol'=32] {'pcol'}, use_global_device_ids=true, to_apply=%region_11.15 | all-reduce | flops 1792 | bytes 14336 | tf_op jit(solution)/shard_map/psum | solution.py:45
  871.3 0.4 fusion.81
  871.8 0.4 fusion.79
  872.2 0.7 abs_reduce_fusion
  872.9 0.6 reshape.376
  873.5 0.6 abs_reduce_fusion.1
  874.1 0.6 copy.40
  874.6 2.2 copy.39
  (88 shorter events, 1.6 us)
Async XLA Ops:
  7.2 47.7 %all-gather.17.cloned.1.call-start = ((), (), s32[]{:S(2)}) async-start(), calls=%async_computation | async-start | bytes 1114112 | tf_op jit(solution)/shard_map/all_gather | solution.py:12
  9.7 1.4 copy-start
  12.6 68.1 %copy-start.1 = (f32[6,128,3,128]{3,1,0,2:T(8,128)}, f32[6,128,3,128]{3,1,0,2:T(8,128)S(1)}, u32[]{:S(2)}) copy-start(f32[6,128,3,128]{3,1,0,2:T(8,128)S(1)} %bitcast_add_fusion) | copy-start | bytes 3538948
  13.4 246.9 %all-gather.19.cloned.1.call-start = ((), (), s32[]{:S(2)}) async-start(), calls=%async_computation.1 | async-start | bytes 12976128 | tf_op jit(solution)/shard_map/all_gather | solution.py:12
  13.4 67.3 %copy-start.19 = (pred[6]{0:T(512)(128)(4,1)}, pred[6]{0:T(512)(128)(4,1)S(1)}, u32[]{:S(2)}) copy-start(pred[6]{0:T(512)(128)(4,1)S(1)} %get-tuple-element.86) | copy-start | bytes 22
  79.4 186.1 %copy-start.2 = (f32[128,128]{1,0:T(8,128)}, f32[128,128]{1,0:T(8,128)S(1)}, u32[]{:S(2)}) copy-start(f32[128,128]{1,0:T(8,128)S(1)} %fusion.52) | copy-start | bytes 196612
  80.7 222.8 %all-gather.21.cloned.1.call-start = ((), (), s32[]{:S(2)}) async-start(), calls=%async_computation.2 | async-start | bytes 3342336 | tf_op jit(solution)/shard_map/all_gather | solution.py:12
  266.9 79.8 %all-gather.23.cloned.1.call-start = ((), (), s32[]{:S(2)}) async-start(), calls=%async_computation.3 | async-start | bytes 1114112 | tf_op jit(solution)/shard_map/all_gather | solution.py:12
  267.0 38.7 %copy-start.16 = (pred[3]{0:T(512)(128)(4,1)}, pred[3]{0:T(512)(128)(4,1)S(1)}, u32[]{:S(2)}) copy-start(pred[3]{0:T(512)(128)(4,1)S(1)} %broadcast_compare_fusion) | copy-start | bytes 13
  308.7 243.3 %all-gather.25.cloned.1.call-start = ((), (), s32[]{:S(2)}) async-start(), calls=%async_computation.4 | async-start | bytes 12976128 | tf_op jit(solution)/shard_map/all_gather | solution.py:12
  309.0 63.5 %copy-start.11 = (pred[6]{0:T(512)(128)(4,1)}, pred[6]{0:T(512)(128)(4,1)S(1)}, u32[]{:S(2)}) copy-start(pred[6]{0:T(512)(128)(4,1)S(1)} %get-tuple-element.87) | copy-start | bytes 22
  309.0 63.5 %copy-start.21 = (pred[6]{0:T(512)(128)(4,1)}, pred[6]{0:T(512)(128)(4,1)S(1)}, u32[]{:S(2)}) copy-start(pred[6]{0:T(512)(128)(4,1)S(1)} %get-tuple-element.88) | copy-start | bytes 22
  371.3 180.8 %copy-start.4 = (f32[128,128]{1,0:T(8,128)}, f32[128,128]{1,0:T(8,128)S(1)}, u32[]{:S(2)}) copy-start(f32[128,128]{1,0:T(8,128)S(1)} %fusion.50) | copy-start | bytes 196612
  372.5 222.8 %all-gather.27.cloned.1.call-start = ((), (), s32[]{:S(2)}) async-start(), calls=%async_computation.5 | async-start | bytes 3342336 | tf_op jit(solution)/shard_map/all_gather | solution.py:12
  552.1 6.7 copy-start.7
  557.4 2.7 copy-start.6
  558.7 2.4 copy-start.17
  558.7 2.4 copy-start.20
  558.8 3.0 copy-start.22
  561.1 0.6 copy-start.13
  599.3 0.7 copy-start.9
  599.3 1.4 copy-start.8
  599.3 31.1 %copy-start.3 = (f32[128,128]{1,0:T(8,128)S(1)}, f32[128,128]{1,0:T(8,128)}, u32[]{:S(2)}) copy-start(f32[128,128]{1,0:T(8,128)} %copy-done.2) | copy-start | bytes 196612
  599.3 113.0 %copy-start.18 = (pred[3]{0:T(512)(128)(4,1)S(1)}, pred[3]{0:T(512)(128)(4,1)}, u32[]{:S(2)}) copy-start(pred[3]{0:T(512)(128)(4,1)} %copy-done.16) | copy-start | bytes 13
  599.4 113.0 %copy-start.5 = (f32[128,128]{1,0:T(8,128)S(1)}, f32[128,128]{1,0:T(8,128)}, u32[]{:S(2)}) copy-start(f32[128,128]{1,0:T(8,128)} %copy-done.4) | copy-start | bytes 196612
  600.7 113.3 %copy-start.10 = (pred[6,3]{0,1:T(4,128)(4,1)S(1)}, pred[6,3]{0,1:T(4,128)(4,1)}, u32[]{:S(2)}) copy-start(pred[6,3]{0,1:T(4,128)(4,1)} %broadcast_and_fusion.1) | copy-start | bytes 58
  714.1 75.4 %copy-start.14 = (pred[3]{0:T(512)(128)(4,1)S(1)}, pred[3]{0:T(512)(128)(4,1)}, u32[]{:S(2)}) copy-start(pred[3]{0:T(512)(128)(4,1)} %copy-done.13) | copy-start | bytes 13
  714.1 75.6 %copy-start.12 = (f32[128]{0:T(128)S(1)}, f32[128]{0:T(128)}, u32[]{:S(2)}) copy-start(f32[128]{0:T(128)} %fusion.13) | copy-start | bytes 1540
  714.1 159.4 %copy-start.15 = (f32[3,128]{1,0:T(4,128)S(1)}, f32[3,128]{1,0:T(4,128)}, u32[]{:S(2)}) copy-start(f32[3,128]{1,0:T(4,128)} %get-tuple-element.76) | copy-start | bytes 4612
Sparse Core Ops, SparseCore 0:
  13.5 41.3 all-gather.16
  80.8 179.3 all-gather.18
  267.0 36.4 all-gather.20
  308.9 37.8 all-gather.22
  372.7 179.3 all-gather.24
  558.8 36.4 all-gather.26
